TPU v7x, 256 devices: a whole 4x4x8 slice. The times are simulated.
256 devices in a mesh: gen: 8 (over z_lo, core), user: 16 (over x, y), cand: 2 (over z_hi).
Axes of the slice: x: 4, y: 4, z: 8 (z_hi: 2, z_lo: 4; z = z_hi * 4 + z_lo), core: 2. Of those that a mesh axis runs over, the one named last changes fastest.
Arguments:
- states: bfloat16 [16384, 4096], P(('user', 'cand')), may hold values from -6 to 6
- norm_gain: float32 [4096], replicated, may hold values from 0.1 to 1.9
- gate_weight: bfloat16 [4096, 7168], P('user', 'gen'), may hold values from -0.09375 to 0.09375
- up_weight: bfloat16 [4096, 7168], P('user', 'gen'), may hold values from -0.09375 to 0.09375
- down_weight: bfloat16 [7168, 4096], P('gen', 'user'), may hold values from -0.0625 to 0.0625
- proj_weight: bfloat16 [4096, 1024], P('gen'), may hold values from -0.09375 to 0.09375
- private_rows: bfloat16 [32768, 1024], P(('gen', 'user')), may hold values from -6 to 6
- enc_weight: bfloat16 [1024, 1024], replicated, may hold values from -0.1875 to 0.1875
- user_ids: int32 [32768], P(('gen', 'user')), may hold values from 0 to 31
Outputs:
- votes: float32 [16, 2, 128], P(None, 'cand')
Inputs may be any that keep to these rules, and one draw needn't show every extreme that they name: `user_ids`: a user is a pair of a block of 256 rows and a slot; no user has rows in two blocks.
All inputs are finite; a program needn't handle non-finite values.
Results may differ from a plain program's by a relative error of at most 0.0025.
Values may be sent and summed in bfloat16 or wider, within the bound.
No kernel may reach another device: no remote copies, remote signals or barrier semaphores. Data moves between devices by JAX's collectives and lax.ppermute only.
A program may use at most 128 MiB of HBM per device.

v0:
```python
import jax
import jax.numpy as jnp
from jax import lax
from jax.sharding import PartitionSpec as P

STEPS = 4
CAP = 8
USERS_DEV = 32


def unit_rows(matrix):
    return (matrix * lax.rsqrt(jnp.sum(matrix * matrix, axis=1, keepdims=True) + 1e-06)).astype(
        jnp.bfloat16
    )


def project_in(inputs, gate_part, up_part):

    def add_rows(piece):
        return jnp.dot(inputs, piece, preferred_element_type=jnp.float32)

    gate = add_rows(lax.all_gather(gate_part, "user", axis=0, tiled=True))
    up_proj = add_rows(lax.all_gather(up_part, "user", axis=0, tiled=True))
    return (gate, up_proj)


def shards(
    states,
    norm_gain,
    gate_weight,
    up_weight,
    down_weight,
    proj_weight,
    private_rows,
    enc_weight,
    user_ids,
):
    tok_rows, width_model = states.shape
    groups = tok_rows // STEPS
    values = states.astype(jnp.float32)
    normed = (
        values * lax.rsqrt(jnp.mean(values * values, axis=1, keepdims=True) + 1e-05) * norm_gain
    ).astype(jnp.bfloat16)
    gate_part, up_part, down_part = (gate_weight, up_weight, down_weight)
    gate, up_proj = project_in(normed, gate_part, up_part)
    hidden = (jax.nn.silu(gate) * up_proj).astype(jnp.bfloat16)
    mixed = jnp.dot(
        hidden,
        lax.all_gather(down_part, "user", axis=1, tiled=True),
        preferred_element_type=jnp.float32,
    )
    pooled_mlp = jnp.sum(mixed.reshape(-1, STEPS, width_model), axis=1)
    pooled_mlp = lax.psum_scatter(pooled_mlp, "gen", scatter_dimension=1, tiled=True)
    slab_width = pooled_mlp.shape[1]
    own_cols = lax.dynamic_slice_in_dim(values, lax.axis_index("gen") * slab_width, slab_width, 1)
    pooled_in = jnp.sum(own_cols.reshape(groups, STEPS, slab_width), axis=1)
    pooled = ((pooled_in + pooled_mlp) / STEPS).astype(jnp.bfloat16)
    partial_emb = jnp.dot(pooled, proj_weight, preferred_element_type=jnp.float32)
    embedding = lax.psum(partial_emb, "gen")
    candidate = unit_rows(embedding)
    every_cand = lax.all_gather(candidate, "user", axis=0, tiled=True)
    encoded = unit_rows(jnp.dot(private_rows, enc_weight, preferred_element_type=jnp.float32))
    scores = lax.dot_general(
        encoded, every_cand, (((1,), (1,)), ((), ())), preferred_element_type=jnp.float32
    )
    kernel = jnp.exp(scores * 60.0)
    totals = lax.psum(jnp.sum(kernel, axis=1), "cand")
    member = (user_ids[:, None] == jnp.arange(USERS_DEV, dtype=jnp.int32)[None, :]).astype(
        jnp.float32
    )
    counts = jnp.sum(member, axis=0)
    limit = jnp.minimum(1.0, CAP / jnp.maximum(counts, 1.0))
    row_cap = jnp.dot(member, limit, precision=lax.Precision.HIGHEST)
    row_total = private_rows.shape[0] * lax.axis_size("gen") * lax.axis_size("user")
    cand_total = every_cand.shape[0] * lax.axis_size("cand")
    weight_rows = row_cap / totals * (cand_total / row_total)
    partial_votes = jnp.dot(weight_rows, kernel, precision=lax.Precision.HIGHEST)
    votes = lax.psum(partial_votes, ("gen", "user"))
    return votes.reshape(lax.axis_size("user"), 1, groups)


def solution(mesh):
    return jax.shard_map(
        shards,
        mesh=mesh,
        in_specs=(
            P(("user", "cand"), None),
            P(),
            P("user", "gen"),
            P("user", "gen"),
            P("gen", "user"),
            P("gen", None),
            P(("gen", "user"), None),
            P(),
            P(("gen", "user")),
        ),
        out_specs=P(None, "cand", None),
        check_vma=False,
    )
```

profile of v0, /device:TPU:0, one launch (start us, length us, event | category | flops | bytes accessed | tf_op | source)
XLA Modules:
  0.0 810.1 jit_solution(10870717847516051505)
XLA Ops:
  6.5 0.0 copy-start
  6.5 0.0 copy-start.1
  6.5 0.0 all-gather.5.cloned.1.call-start
  6.5 0.7 all-gather.5.cloned.1.call-update
  7.3 0.0 all-gather.7.cloned.1.call-start
  7.3 0.7 all-gather.7.cloned.1.call-update
  8.0 0.0 all-gather.9.cloned.1.call-start
  8.1 0.7 all-gather.9.cloned.1.call-update
  8.7 0.0 reduce-scatter.2.cloned.1.call-start
  8.8 3.1 multiply_reduce_fusion
  11.9 70.3 %all-gather.5.cloned.1.call-done = bf16[4096,896]{1,0:T(8,128)(2,1)} async-done(((bf16[256,896]{1,0:T(8,128)(2,1)}), bf16[4096,896]{1,0:T(8,128)(2,1)}) %all-gather.5.cloned.1.call-update) | async-done | bytes 7340048 | tf_op jit(solution)/shard_map/all_gather | solution.py:22
  82.2 0.0 copy-done.1
  82.2 10.1 %fusion.1 = f32[512,896]{1,0:T(8,128)} fusion(bf16[4096,896]{1,0:T(8,128)(2,1)} %all-gather.5.cloned.1.call-done, f32[4096]{0:T(1024)S(1)} %copy-done.1, f32[512]{0:T(512)S(1)} %add_rsqrt_fusion, bf16[512,4096]{1,0:T(8,128)(2,1)} %param.9), kind=kOutput, calls=%fused_computation.5 | convolution fusion | flops 3766484992 | bytes 13387776 | tf_op jit(solution)/shard_map/dot_general | solution.py:20
  92.3 63.2 %all-gather.7.cloned.1.call-done = bf16[4096,896]{1,0:T(8,128)(2,1)} async-done(((bf16[256,896]{1,0:T(8,128)(2,1)}), bf16[4096,896]{1,0:T(8,128)(2,1)}) %all-gather.7.cloned.1.call-update) | async-done | bytes 7340048 | tf_op jit(solution)/shard_map/all_gather | solution.py:23
  155.6 79.3 %all-gather.9.cloned.1.call-done = bf16[896,4096]{1,0:T(8,128)(2,1)} async-done(((bf16[896,256]{1,0:T(8,128)(2,1)}), bf16[896,4096]{1,0:T(8,128)(2,1)}) %all-gather.9.cloned.1.call-update) | async-done | bytes 7340048 | tf_op jit(solution)/shard_map/all_gather | solution.py:49
  234.8 17.4 %fusion.2 = f32[512,4096]{1,0:T(8,128)} fusion(bf16[896,4096]{1,0:T(8,128)(2,1)} %all-gather.9.cloned.1.call-done, f32[512,896]{1,0:T(8,128)} %fusion.1, bf16[4096,896]{1,0:T(8,128)(2,1)} %all-gather.7.cloned.1.call-done, f32[4096]{0:T(1024)S(1)} %copy-done.1, f32[512]{0:T(512)S(1)} %add_rsqrt_fusion, bf16[512,4096]{1,0:T(8,128)(2,1)} %param.9), kind=kOutput, calls=%fused_computation.9 | convolution fusion | flops 7527333888 | bytes 29116416 | tf_op jit(solution)/shard_map/dot_general | solution.py:47
  252.2 9.8 %reshape.32 = f32[128,4,4096]{2,1,0:T(4,128)} reshape(f32[512,4096]{1,0:T(8,128)} %fusion.2) | data formatting | bytes 16777216 | tf_op jit(solution)/shard_map/reshape | solution.py:52
  262.0 10.0 %reduce_sum.67 = f32[128,4096]{1,0:T(8,128)} reduce(f32[128,4,4096]{2,1,0:T(4,128)} %reshape.32, f32[]{:T(128)} %constant.15.clone.1), dimensions={1}, to_apply=%region_4.5 | reduce | flops 1572864 | bytes 10485764 | tf_op jit(solution)/shard_map/reduce_sum | solution.py:52
  272.0 0.0 reduce-scatter.2.cloned.1.call-update
  272.1 0.0 all-reduce.2.cloned.1.call-start
  272.1 6.5 convert_element_type.23
  278.6 1.3 constant_dynamic-slice_fusion
  279.9 0.0 copy-start.2
  279.9 1.3 reshape.31
  281.2 1.8 reduce_sum.65
  283.1 29.9 %reduce-scatter.2.cloned.1.call-done = f32[128,512]{1,0:T(8,128)} async-done(((f32[128,4096]{1,0:T(8,128)}), f32[128,512]{1,0:T(8,128)}) %reduce-scatter.2.cloned.1.call-update) | async-done | bytes 262160 | tf_op jit(solution)/shard_map/reduce_scatter | solution.py:53
  313.0 2.4 fusion.4
  315.4 0.0 all-reduce.2.cloned.1.call-update
  315.4 0.3 all-gather.11.cloned.1.call-start
  315.7 70.7 %all-reduce.2.cloned.1.call-done = f32[128,1024]{1,0:T(8,128)} async-done(((f32[128,1024]{1,0:T(8,128)}), f32[128,1024]{1,0:T(8,128)}) %all-reduce.2.cloned.1.call-update) | async-done | bytes 524304 | tf_op jit(solution)/shard_map/psum | solution.py:59
  386.3 1.2 multiply_reduce_fusion.2
  387.5 1.8 multiply_convert_fusion.8
  389.3 0.0 all-gather.11.cloned.1.call-update
  389.4 0.0 copy-done.2
  389.4 0.1 convert_reduce_fusion
  389.5 0.0 copy-done
  389.5 1.8 multiply_reduce_fusion.1
  391.3 0.1 fusion.6
  391.5 53.5 %all-gather.11.cloned.1.call-done = bf16[2048,1024]{1,0:T(8,128)(2,1)} async-done(((bf16[128,1024]{1,0:T(8,128)(2,1)}), bf16[2048,1024]{1,0:T(8,128)(2,1)}) %all-gather.11.cloned.1.call-update) | async-done | bytes 4194320 | tf_op jit(solution)/shard_map/all_gather | solution.py:61
  445.0 4.9 fusion.16
  449.8 8.8 %psum.22 = f32[256]{0:T(256)S(1)} all-reduce(f32[256]{0:T(256)S(1)} %get-tuple-element.7), channel_id=1, replica_groups=mesh['gen'=8,'user'=16,'cand'=2] {'cand'}, use_global_device_ids=true, to_apply=%region_9.10 | all-reduce | flops 256 | bytes 2048 | tf_op jit(solution)/shard_map/psum | solution.py:67
  458.6 2.7 convolution_bitcast_fusion
  461.3 341.9 %psum.23 = f32[16,1,128]{2,1,0:T(1,128)} all-reduce(f32[16,1,128]{2,1,0:T(1,128)S(1)} %convolution_bitcast_fusion), channel_id=1, replica_groups=mesh['gen'=8,'user'=16,'cand'=2] {'gen','user'}, use_global_device_ids=true, to_apply=%region_10.11 | all-reduce | flops 2048 | bytes 16384 | tf_op jit(solution)/shard_map/psum | solution.py:78
  (4 shorter events, 0.0 us)
Async XLA Ops:
  6.5 383.0 %copy-start = (bf16[1024,1024]{1,0:T(8,128)(2,1)S(1)}, bf16[1024,1024]{1,0:T(8,128)(2,1)}, u32[]{:S(2)}) copy-start(bf16[1024,1024]{1,0:T(8,128)(2,1)} %param.16) | copy-start | bytes 6291460
  6.5 75.7 %copy-start.1 = (f32[4096]{0:T(1024)S(1)}, f32[4096]{0:T(1024)}, u32[]{:S(2)}) copy-start(f32[4096]{0:T(1024)} %param.10) | copy-start | bytes 49156
  6.5 75.7 %all-gather.5.cloned.1.call-start = ((), (), s32[]{:S(2)}) async-start(), calls=%async_computation.1 | async-start | bytes 7798784 | tf_op jit(solution)/shard_map/all_gather | solution.py:22
  7.3 148.3 %all-gather.7.cloned.1.call-start = ((), (), s32[]{:S(2)}) async-start(), calls=%async_computation.2 | async-start | bytes 7798784 | tf_op jit(solution)/shard_map/all_gather | solution.py:23
  8.0 226.8 %all-gather.9.cloned.1.call-start = ((), (), s32[]{:S(2)}) async-start(), calls=%async_computation.3 | async-start | bytes 7798784 | tf_op jit(solution)/shard_map/all_gather | solution.py:49
  8.7 304.2 %reduce-scatter.2.cloned.1.call-start = ((), (), s32[]{:S(2)}) async-start(), calls=%async_computation.4 | async-start | bytes 2359296 | tf_op jit(solution)/shard_map/reduce_scatter | solution.py:53
  272.1 114.3 %all-reduce.2.cloned.1.call-start = ((), (), s32[]{:S(2)}) async-start(), calls=%async_computation.5 | async-start | bytes 1048576 | tf_op jit(solution)/shard_map/psum | solution.py:59
  279.9 109.5 %copy-start.2 = (s32[256]{0:T(256)S(1)}, s32[256]{0:T(256)}, u32[]{:S(2)}) copy-start(s32[256]{0:T(256)} %param.17) | copy-start | bytes 3076
  315.4 129.5 %all-gather.11.cloned.1.call-start = ((), (), s32[]{:S(2)}) async-start(), calls=%async_computation.6 | async-start | bytes 4456448 | tf_op jit(solution)/shard_map/all_gather | solution.py:61
Sparse Core Ops, SparseCore 0:
  9.8 72.3 all-gather.4
  84.7 70.8 all-gather.6
  158.0 76.7 all-gather.8
  272.2 40.7 reduce-scatter.1
  315.5 70.7 all-reduce.1
  389.5 55.4 all-gather.10
where the time goes:
time: 811 us; the launch traced here: 810 us
  waiting for transfers between devices  369 us (45%)
  blocking collectives  351 us (43%)
  matrix products  39.5 us (5%)
  other arithmetic  24.6 us (3%)
  between operations  13.5 us (2%)
  local copies, waits for them, and re-layouts  12.4 us (2%)
    psum x1, blocking collectives, shards(): votes = lax.psum(partial_votes, ('gen', 'user'))  342 us
    all_gather x1, waiting for transfers between devices, shards(): lax.all_gather(down_part, 'user', axis=1, tiled=True)  79.3 us
    psum x1, waiting for transfers between devices, shards(): embedding = lax.psum(partial_emb, 'gen')  70.7 us
    all_gather x1, waiting for transfers between devices, project_in(): gate = add_rows(lax.all_gather(gate_part, 'user', axis=0, tiled=True))  70.3 us
    all_gather x1, waiting for transfers between devices, project_in(): up_proj = add_rows(lax.all_gather(up_part, 'user', axis=0, tiled=True))  63.2 us
    all_gather x1, waiting for transfers between devices, shards(): every_cand = lax.all_gather(candidate, 'user', axis=0, tiled=True)  53.5 us
    reduce_scatter x1, waiting for transfers between devices, shards(): lax.psum_scatter(pooled_mlp, 'gen', scatter_dimension=1, tiled=True)  29.9 us
    dot_general x1, matrix products, shards(): jnp.dot(hidden, lax.all_gather(down_part, 'user', axis=1, tiled=True), pr...  17.4 us
  transfers between devices with their start and end apart: 6, of which 6 were waited for; matrix products, arithmetic and copies ran while one was open for 3% of the time, Pallas kernels for 0%

commit v1 on v0

--- a/solution.py
+++ b/solution.py
@@ -75,7 +75,9 @@
     cand_total = every_cand.shape[0] * lax.axis_size("cand")
     weight_rows = row_cap / totals * (cand_total / row_total)
     partial_votes = jnp.dot(weight_rows, kernel, precision=lax.Precision.HIGHEST)
-    votes = lax.psum(partial_votes, ("gen", "user"))
+    votes = partial_votes
+    for mesh_axis in ("user", "gen"):
+        votes = lax.psum(votes, mesh_axis)
     return votes.reshape(lax.axis_size("user"), 1, groups)
 
 

time: 811 us -> 525 us (0.65)
  blocking collectives: 351 us -> 62.2 us
    psum x1 -> x2, blocking collectives: 342 us -> 53.3 us  [shards(): votes = lax.psum(votes, mesh_axis)]
  transfers between devices with their start and end apart: 6 -> 6, of which waited for: 6 -> 6; matrix products, arithmetic and copies ran while one was open for 3% -> 5% of each run, Pallas kernels for 0% -> 0%
where the time goes in v1:
time: 525 us; the launch traced here: 522 us
  waiting for transfers between devices  369 us (70%)
  blocking collectives  62.2 us (12%)
  matrix products  39.5 us (8%)
  other arithmetic  24.6 us (5%)
  between operations  13.5 us (3%)
  local copies, waits for them, and re-layouts  12.4 us (2%)
    all_gather x1, waiting for transfers between devices, shards(): lax.all_gather(down_part, 'user', axis=1, tiled=True)  79.3 us
    psum x1, waiting for transfers between devices, shards(): embedding = lax.psum(partial_emb, 'gen')  70.7 us
    all_gather x1, waiting for transfers between devices, project_in(): gate = add_rows(lax.all_gather(gate_part, 'user', axis=0, tiled=True))  70.3 us
    all_gather x1, waiting for transfers between devices, project_in(): up_proj = add_rows(lax.all_gather(up_part, 'user', axis=0, tiled=True))  63.2 us
    all_gather x1, waiting for transfers between devices, shards(): every_cand = lax.all_gather(candidate, 'user', axis=0, tiled=True)  53.5 us
    psum x2, blocking collectives, shards(): votes = lax.psum(votes, mesh_axis)  53.3 us
    reduce_scatter x1, waiting for transfers between devices, shards(): lax.psum_scatter(pooled_mlp, 'gen', scatter_dimension=1, tiled=True)  29.9 us
    dot_general x1, matrix products, shards(): jnp.dot(hidden, lax.all_gather(down_part, 'user', axis=1, tiled=True), pr...  17.4 us
  transfers between devices with their start and end apart: 6, of which 6 were waited for; matrix products, arithmetic and copies ran while one was open for 5% of the time, Pallas kernels for 0%

profile of v1, /device:TPU:0, one launch (start us, length us, event | category | flops | bytes accessed | tf_op | source)
XLA Modules:
  0.0 521.5 jit_solution(14013411171418830363)
XLA Ops:
  6.5 0.0 copy-start
  6.5 0.0 copy-start.1
  6.5 0.0 all-gather.5.cloned.1.call-start
  6.5 0.7 all-gather.5.cloned.1.call-update
  7.3 0.0 all-gather.7.cloned.1.call-start
  7.3 0.7 all-gather.7.cloned.1.call-update
  8.0 0.0 all-gather.9.cloned.1.call-start
  8.1 0.7 all-gather.9.cloned.1.call-update
  8.7 0.0 reduce-scatter.2.cloned.1.call-start
  8.8 3.1 multiply_reduce_fusion
  11.9 70.3 %all-gather.5.cloned.1.call-done = bf16[4096,896]{1,0:T(8,128)(2,1)} async-done(((bf16[256,896]{1,0:T(8,128)(2,1)}), bf16[4096,896]{1,0:T(8,128)(2,1)}) %all-gather.5.cloned.1.call-update) | async-done | bytes 7340048 | tf_op jit(solution)/shard_map/all_gather | solution.py:22
  82.2 0.0 copy-done.1
  82.2 10.1 %fusion.1 = f32[512,896]{1,0:T(8,128)} fusion(bf16[4096,896]{1,0:T(8,128)(2,1)} %all-gather.5.cloned.1.call-done, f32[4096]{0:T(1024)S(1)} %copy-done.1, f32[512]{0:T(512)S(1)} %add_rsqrt_fusion, bf16[512,4096]{1,0:T(8,128)(2,1)} %param.9), kind=kOutput, calls=%fused_computation.5 | convolution fusion | flops 3766484992 | bytes 13387776 | tf_op jit(solution)/shard_map/dot_general | solution.py:20
  92.3 63.2 %all-gather.7.cloned.1.call-done = bf16[4096,896]{1,0:T(8,128)(2,1)} async-done(((bf16[256,896]{1,0:T(8,128)(2,1)}), bf16[4096,896]{1,0:T(8,128)(2,1)}) %all-gather.7.cloned.1.call-update) | async-done | bytes 7340048 | tf_op jit(solution)/shard_map/all_gather | solution.py:23
  155.6 79.3 %all-gather.9.cloned.1.call-done = bf16[896,4096]{1,0:T(8,128)(2,1)} async-done(((bf16[896,256]{1,0:T(8,128)(2,1)}), bf16[896,4096]{1,0:T(8,128)(2,1)}) %all-gather.9.cloned.1.call-update) | async-done | bytes 7340048 | tf_op jit(solution)/shard_map/all_gather | solution.py:49
  234.8 17.4 %fusion.2 = f32[512,4096]{1,0:T(8,128)} fusion(bf16[896,4096]{1,0:T(8,128)(2,1)} %all-gather.9.cloned.1.call-done, f32[512,896]{1,0:T(8,128)} %fusion.1, bf16[4096,896]{1,0:T(8,128)(2,1)} %all-gather.7.cloned.1.call-done, f32[4096]{0:T(1024)S(1)} %copy-done.1, f32[512]{0:T(512)S(1)} %add_rsqrt_fusion, bf16[512,4096]{1,0:T(8,128)(2,1)} %param.9), kind=kOutput, calls=%fused_computation.8 | convolution fusion | flops 7527333888 | bytes 29116416 | tf_op jit(solution)/shard_map/dot_general | solution.py:47
  252.2 9.8 %reshape.32 = f32[128,4,4096]{2,1,0:T(4,128)} reshape(f32[512,4096]{1,0:T(8,128)} %fusion.2) | data formatting | bytes 16777216 | tf_op jit(solution)/shard_map/reshape | solution.py:52
  262.0 10.0 %reduce_sum.67 = f32[128,4096]{1,0:T(8,128)} reduce(f32[128,4,4096]{2,1,0:T(4,128)} %reshape.32, f32[]{:T(128)} %constant.15.clone.1), dimensions={1}, to_apply=%region_4.5 | reduce | flops 1572864 | bytes 10485764 | tf_op jit(solution)/shard_map/reduce_sum | solution.py:52
  272.0 0.0 reduce-scatter.2.cloned.1.call-update
  272.1 0.0 all-reduce.2.cloned.1.call-start
  272.1 6.5 %convert_element_type.23 = f32[512,4096]{1,0:T(8,128)} convert(bf16[512,4096]{1,0:T(8,128)(2,1)} %param.9) | non-fusion elementwise | flops 2097152 | bytes 12582912 | tf_op jit(solution)/shard_map/convert_element_type | solution.py:40
  278.6 1.3 constant_dynamic-slice_fusion
  279.9 0.0 copy-start.2
  279.9 1.3 reshape.31
  281.2 1.8 reduce_sum.65
  283.1 29.9 %reduce-scatter.2.cloned.1.call-done = f32[128,512]{1,0:T(8,128)} async-done(((f32[128,4096]{1,0:T(8,128)}), f32[128,512]{1,0:T(8,128)}) %reduce-scatter.2.cloned.1.call-update) | async-done | bytes 262160 | tf_op jit(solution)/shard_map/reduce_scatter | solution.py:53
  313.0 2.4 fusion.4
  315.4 0.0 all-reduce.2.cloned.1.call-update
  315.4 0.3 all-gather.11.cloned.1.call-start
  315.7 70.7 %all-reduce.2.cloned.1.call-done = f32[128,1024]{1,0:T(8,128)} async-done(((f32[128,1024]{1,0:T(8,128)}), f32[128,1024]{1,0:T(8,128)}) %all-reduce.2.cloned.1.call-update) | async-done | bytes 524304 | tf_op jit(solution)/shard_map/psum | solution.py:59
  386.3 1.2 multiply_reduce_fusion.2
  387.5 1.8 multiply_convert_fusion.8
  389.3 0.0 all-gather.11.cloned.1.call-update
  389.4 0.0 copy-done.2
  389.4 0.1 convert_reduce_fusion
  389.5 0.0 copy-done
  389.5 1.8 multiply_reduce_fusion.1
  391.3 0.1 fusion.6
  391.5 53.5 %all-gather.11.cloned.1.call-done = bf16[2048,1024]{1,0:T(8,128)(2,1)} async-done(((bf16[128,1024]{1,0:T(8,128)(2,1)}), bf16[2048,1024]{1,0:T(8,128)(2,1)}) %all-gather.11.cloned.1.call-update) | async-done | bytes 4194320 | tf_op jit(solution)/shard_map/all_gather | solution.py:61
  445.0 4.9 fusion.16
  449.8 8.8 %psum.29 = f32[256]{0:T(256)S(1)} all-reduce(f32[256]{0:T(256)S(1)} %get-tuple-element.7), channel_id=1, replica_groups=mesh['gen'=8,'user'=16,'cand'=2] {'cand'}, use_global_device_ids=true, to_apply=%region_9.10 | all-reduce | flops 256 | bytes 2048 | tf_op jit(solution)/shard_map/psum | solution.py:67
  458.6 2.7 fusion.17
  461.3 38.9 %psum.30 = f32[2048]{0:T(1024)S(1)} all-reduce(f32[2048]{0:T(1024)S(1)} %bitcast.16), channel_id=1, replica_groups=mesh['gen'=8,'user'=16,'cand'=2] {'user'}, use_global_device_ids=true, to_apply=%region_10.11 | all-reduce | flops 2048 | bytes 16384 | tf_op jit(solution)/shard_map/psum | solution.py:80
  500.3 14.4 %psum.31 = f32[16,1,128]{2,1,0:T(1,128)} all-reduce(f32[16,1,128]{2,1,0:T(1,128)S(1)} %bitcast.17), channel_id=1, replica_groups=mesh['gen'=8,'user'=16,'cand'=2] {'gen'}, use_global_device_ids=true, to_apply=%region_11.12 | all-reduce | flops 2048 | bytes 16384 | tf_op jit(solution)/shard_map/psum | solution.py:80
  (4 shorter events, 0.0 us)
Async XLA Ops:
  6.5 383.0 %copy-start = (bf16[1024,1024]{1,0:T(8,128)(2,1)S(1)}, bf16[1024,1024]{1,0:T(8,128)(2,1)}, u32[]{:S(2)}) copy-start(bf16[1024,1024]{1,0:T(8,128)(2,1)} %param.16) | copy-start | bytes 6291460
  6.5 75.7 %copy-start.1 = (f32[4096]{0:T(1024)S(1)}, f32[4096]{0:T(1024)}, u32[]{:S(2)}) copy-start(f32[4096]{0:T(1024)} %param.10) | copy-start | bytes 49156
  6.5 75.7 %all-gather.5.cloned.1.call-start = ((), (), s32[]{:S(2)}) async-start(), calls=%async_computation.1 | async-start | bytes 7798784 | tf_op jit(solution)/shard_map/all_gather | solution.py:22
  7.3 148.3 %all-gather.7.cloned.1.call-start = ((), (), s32[]{:S(2)}) async-start(), calls=%async_computation.2 | async-start | bytes 7798784 | tf_op jit(solution)/shard_map/all_gather | solution.py:23
  8.0 226.8 %all-gather.9.cloned.1.call-start = ((), (), s32[]{:S(2)}) async-start(), calls=%async_computation.3 | async-start | bytes 7798784 | tf_op jit(solution)/shard_map/all_gather | solution.py:49
  8.7 304.2 %reduce-scatter.2.cloned.1.call-start = ((), (), s32[]{:S(2)}) async-start(), calls=%async_computation.4 | async-start | bytes 2359296 | tf_op jit(solution)/shard_map/reduce_scatter | solution.py:53
  272.1 114.3 %all-reduce.2.cloned.1.call-start = ((), (), s32[]{:S(2)}) async-start(), calls=%async_computation.5 | async-start | bytes 1048576 | tf_op jit(solution)/shard_map/psum | solution.py:59
  279.9 109.5 %copy-start.2 = (s32[256]{0:T(256)S(1)}, s32[256]{0:T(256)}, u32[]{:S(2)}) copy-start(s32[256]{0:T(256)} %param.17) | copy-start | bytes 3076
  315.4 129.5 %all-gather.11.cloned.1.call-start = ((), (), s32[]{:S(2)}) async-start(), calls=%async_computation.6 | async-start | bytes 4456448 | tf_op jit(solution)/shard_map/all_gather | solution.py:61
Sparse Core Ops, SparseCore 0:
  9.8 72.3 all-gather.4
  84.7 70.8 all-gather.6
  158.0 76.7 all-gather.8
  272.2 40.7 reduce-scatter.1
  315.5 70.7 all-reduce.1
  389.5 55.4 all-gather.10
